TPU v7x, 256 devices: a whole 4x4x8 slice. The times are simulated.
256 devices in a mesh: row: 32 (over y, z), col: 8 (over x, core).
Axes of the slice: x: 4, y: 4, z: 8, core: 2. Of those that a mesh axis runs over, the one named last changes fastest.
Arguments:
- panel_one: bfloat16 [512, 32768], P('col', 'row'), may hold values from -1.1953125 to 1.1953125
- panel_two: bfloat16 [512, 32768], P('col', 'row'), may hold values from -3 to 3
- inverse_one: bfloat16 [512, 512], replicated
- inverse_two: bfloat16 [512, 512], replicated
- column_blocks: int32 [4], replicated, may hold values from 0 to 255, as said below
- row_map: int32 [256], P('row'), may hold values from 0 to 255, as said below
- targets: bfloat16 [32, 8, 128, 128, 128], P('row', 'col'), may hold values from -6 to 6
- rows_one: int32 [32, 8, 128], P('row', 'col'), may hold values from 0 to 255, as said below
- cols_one: int32 [32, 8, 128], P('row', 'col'), may hold values from 0 to 255, as said below
- rows_two: int32 [32, 8, 128], P('row', 'col'), may hold values from 0 to 255, as said below
- cols_two: int32 [32, 8, 128], P('row', 'col'), may hold values from 0 to 255, as said below
Outputs:
- lower_one: bfloat16 [512, 32768], P('col', 'row')
- lower_two: bfloat16 [512, 32768], P('col', 'row')
- trailing: bfloat16 [32, 8, 128, 128, 128], P('row', 'col')
Inputs may be any that keep to these rules, and one draw needn't show every extreme that they name: `column_blocks`: the entries are distinct. row_map[j] // 8 equals j // 8; within each aligned run of 8 entries every value of the run appears once. rows_one[r, c, s] // 8 equals r. cols_one[r, c, s] % 8 equals c. rows_two[r, c, s] // 8 equals r. cols_two[r, c, s] % 8 equals c.
All inputs are finite; a program needn't handle non-finite values.
Results may differ from a plain program's by a relative error of at most 0.006.
Values may be sent and summed in bfloat16 or wider, within the bound.
A program may use at most 192 MiB of HBM per device.

v0:
```python
import jax
import jax.numpy as jnp
from jax import lax
from jax.sharding import PartitionSpec as P


def factor_panel(panel_part, inverse):
    summed = jnp.dot(
        inverse,
        lax.all_gather(panel_part, "col", axis=0, tiled=True),
        preferred_element_type=jnp.float32,
    )
    return summed.astype(jnp.bfloat16)


def bridge_columns(lower_full, column_blocks, slab_rows, block_size):
    local_count = lower_full.shape[1] // block_size
    begin_col = lax.axis_index("col") * slab_rows
    chosen = column_blocks[begin_col // block_size]
    offset = begin_col % block_size
    column_piece = lax.dynamic_slice_in_dim(
        lower_full, chosen % local_count * block_size + offset, slab_rows, 1
    )
    owner_row = chosen // local_count
    owned_here = owner_row == lax.axis_index("row")
    summed = lax.psum(
        jnp.where(owned_here, column_piece.astype(jnp.float32), 0.0).astype(jnp.bfloat16), "row"
    )
    return summed


def pick_tiles(lower_full, block_size):
    col_count = lax.axis_size("col")
    panel_width, row_count = lower_full.shape
    grouped = lower_full.reshape(
        panel_width, row_count // (block_size * col_count), col_count, block_size
    )
    chosen = lax.dynamic_index_in_dim(grouped, lax.axis_index("col"), 2, keepdims=False)
    return chosen.reshape(panel_width, -1)


def gather_tiles(lower_full, block_size):
    return lax.all_gather(pick_tiles(lower_full, block_size), "row", axis=1, tiled=True)


def schur_terms(lower_full, tiles, slot_rows, slot_cols, block_size):
    panel_width = lower_full.shape[0]
    local_blocks = lower_full.reshape(panel_width, -1, block_size)
    column_set = tiles.reshape(panel_width, -1, block_size)
    local_count = local_blocks.shape[1]
    left_tiles = jnp.take(local_blocks, slot_rows.reshape(-1) % local_count, axis=1)
    right_tiles = jnp.take(column_set, slot_cols.reshape(-1) // lax.axis_size("col"), axis=1)
    return jnp.einsum("wsx,wsy->sxy", left_tiles, right_tiles, preferred_element_type=jnp.float32)


def own_slice(lower_full, slab_rows):
    return lax.dynamic_slice_in_dim(lower_full, lax.axis_index("col") * slab_rows, slab_rows, 0)


def per_device(
    panel_one,
    panel_two,
    inverse_one,
    inverse_two,
    column_blocks,
    row_map,
    targets,
    rows_one,
    cols_one,
    rows_two,
    cols_two,
):
    block_size = targets.shape[-1]
    slab_rows = panel_one.shape[0]
    panel_width = inverse_one.shape[0]
    row_count = panel_one.shape[1]
    local_count = row_count // block_size
    lower_one = factor_panel(panel_one, inverse_one)
    blocks_one = lower_one.reshape(panel_width, local_count, block_size)
    bridge = bridge_columns(lower_one, column_blocks, slab_rows, block_size)
    mapped = jnp.take(blocks_one, row_map % local_count, axis=1).reshape(panel_width, row_count)
    update = lax.dot_general(
        bridge, mapped, (((0,), (0,)), ((), ())), preferred_element_type=jnp.float32
    )
    updated = (panel_two.astype(jnp.float32) - update).astype(jnp.bfloat16)
    lower_two = factor_panel(updated, inverse_two)
    tiles_one = gather_tiles(lower_one, block_size)
    tiles_two = gather_tiles(lower_two, block_size)
    terms = schur_terms(lower_one, tiles_one, rows_one, cols_one, block_size)
    terms = terms + schur_terms(lower_two, tiles_two, rows_two, cols_two, block_size)
    trailing = (
        (targets.astype(jnp.float32).reshape(terms.shape) - terms)
        .astype(jnp.bfloat16)
        .reshape(targets.shape)
    )
    return (own_slice(lower_one, slab_rows), own_slice(lower_two, slab_rows), trailing)


def solution(mesh):
    return jax.shard_map(
        per_device,
        mesh=mesh,
        in_specs=(
            P("col", "row"),
            P("col", "row"),
            P(),
            P(),
            P(),
            P("row"),
            P("row", "col", None, None, None),
            P("row", "col", None),
            P("row", "col", None),
            P("row", "col", None),
            P("row", "col", None),
        ),
        out_specs=(P("col", "row"), P("col", "row"), P("row", "col", None, None, None)),
        check_vma=False,
    )
```

profile of v0, /device:TPU:2, one launch (start us, length us, event | category | flops | bytes accessed | tf_op | source)
XLA Modules:
  0.0 418.5 jit_solution(15414585895211025504)
XLA Ops:
  8.0 1.2 dynamic_slice.20
  12.7 24.4 %all-gather.7.cloned.1.call-done = bf16[512,1024]{1,0:T(8,128)(2,1)} async-done(((bf16[64,1024]{1,0:T(8,128)(2,1)}), bf16[512,1024]{1,0:T(8,128)(2,1)}) %all-gather.7.cloned.1.call-update) | async-done | bytes 1048592 | tf_op jit(solution)/shard_map/all_gather | solution.py:10
  37.1 1.9 convolution_convert_fusion.1
  39.2 0.8 select_convert_fusion
  40.1 1.7 gather_fusion
  41.7 2.3 copy.22
  44.0 2.4 bitcast_select_fusion
  46.4 138.7 %all-reduce.2.cloned.1.call-done = bf16[512,64]{1,0:T(8,128)(2,1)} async-done(((bf16[512,64]{1,0:T(8,128)(2,1)}), bf16[512,64]{1,0:T(8,128)(2,1)}) %all-reduce.2.cloned.1.call-update) | async-done | bytes 65552 | tf_op jit(solution)/shard_map/psum | solution.py:26
  185.1 2.4 fusion.23
  187.5 1.3 copy.30
  188.9 1.6 constant_dynamic-slice_fusion.1
  190.7 19.4 %all-gather.9.cloned.1.call-done = bf16[512,1024]{1,0:T(8,128)(2,1)} async-done(((bf16[64,1024]{1,0:T(8,128)(2,1)}), bf16[512,1024]{1,0:T(8,128)(2,1)}) %all-gather.9.cloned.1.call-update) | async-done | bytes 1048592 | tf_op jit(solution)/shard_map/all_gather | solution.py:10
  210.1 2.1 convolution_convert_fusion
  213.1 8.2 %gather_fusion.1 = bf16[128,512,128]{2,1,0:T(8,128)(2,1)} fusion(bf16[512,8,128]{2,0,1:T(8,128)(2,1)S(1)} %copy_bitcast_fusion, s32[1024]{0:T(1024)S(1)} %pad_clamp_fusion.3), kind=kCustom, calls=%fused_computation.clone | custom fusion | bytes 33554944 | tf_op jit(solution)/shard_map/jit(_take)/gather | solution.py:51
  221.3 1.6 constant_dynamic-slice_fusion.2
  223.8 8.2 %gather_fusion.3 = bf16[128,512,128]{1,2,0:T(8,128)(2,1)} fusion(bf16[512,8,128]{0,2,1:T(8,128)(2,1)S(1)} %bitcast.77, s32[1024]{0:T(1024)S(1)} %pad_clamp_fusion.1), kind=kCustom, calls=%fused_computation.2.clone | custom fusion | bytes 33554944 | tf_op jit(solution)/shard_map/jit(_take)/gather | solution.py:51
  232.1 63.8 %all-gather.11.cloned.1.call-done = bf16[512,1,1,4096]{0,3,2,1:T(8,128)(2,1)} async-done(((bf16[512,1,1,128]{0,3,2,1:T(8,128)(2,1)}), bf16[512,1,1,4096]{0,3,2,1:T(8,128)(2,1)}) %all-gather.11.cloned.1.call-update) | async-done | bytes 4194320 | tf_op jit(solution)/shard_map/all_gather | solution.py:43
  295.9 6.4 %copy.25 = bf16[512,32,128]{2,0,1:T(8,128)(2,1)} copy(bf16[512,32,128]{0,2,1:T(8,128)(2,1)} %bitcast.79) | data formatting | bytes 8388608 | tf_op jit(solution)/shard_map/reshape | solution.py:49
  302.3 10.6 %gather_fusion.2 = bf16[128,512,128]{2,1,0:T(8,128)(2,1)} fusion(bf16[512,32,128]{2,0,1:T(8,128)(2,1)} %copy.25, s32[1024]{0:T(1024)S(1)} %pad_clamp_fusion.2), kind=kCustom, calls=%fused_computation.1.clone | custom fusion | bytes 33554944 | tf_op jit(solution)/shard_map/jit(_take)/gather | solution.py:52
  312.9 16.8 %fusion.3 = f32[128,128,128]{2,1,0:T(8,128)} fusion(bf16[128,512,128]{2,1,0:T(8,128)(2,1)} %gather_fusion.2, bf16[128,512,128]{2,1,0:T(8,128)(2,1)} %gather_fusion.1, pred[128]{0:T(512)(128)(4,1)S(1)} %get-tuple-element.20, pred[128]{0:T(512)(128)(4,1)S(1)} %get-tuple-element.26), kind=kOutput, calls=%fused_computation.8 | convolution fusion | flops 2164260864 | bytes 41943296 | tf_op jit(solution)/shard_map/wsx,wsy->sxy/dot_general | solution.py:53
  329.7 47.2 %all-gather.13.cloned.1.call-done = bf16[512,1,1,4096]{0,3,2,1:T(8,128)(2,1)} async-done(((bf16[512,1,1,128]{0,3,2,1:T(8,128)(2,1)}), bf16[512,1,1,4096]{0,3,2,1:T(8,128)(2,1)}) %all-gather.13.cloned.1.call-update) | async-done | bytes 4194320 | tf_op jit(solution)/shard_map/all_gather | solution.py:43
  376.9 6.4 %copy.27 = bf16[512,32,128]{2,0,1:T(8,128)(2,1)} copy(bf16[512,32,128]{0,2,1:T(8,128)(2,1)} %bitcast.80) | data formatting | bytes 8388608 | tf_op jit(solution)/shard_map/reshape | solution.py:49
  383.3 10.5 %gather_fusion.4 = bf16[128,512,128]{2,1,0:T(8,128)(2,1)} fusion(bf16[512,32,128]{2,0,1:T(8,128)(2,1)} %copy.27, s32[1024]{0:T(1024)S(1)} %pad_clamp_fusion), kind=kCustom, calls=%fused_computation.3.clone | custom fusion | bytes 33554944 | tf_op jit(solution)/shard_map/jit(_take)/gather | solution.py:52
  393.8 18.2 %fusion.18 = bf16[1,1,128,128,128]{4,3,2,1,0:T(8,128)(2,1)} fusion(f32[128,128,128]{2,1,0:T(8,128)} %fusion.3, bf16[1,1,128,128,128]{4,3,2,1,0:T(8,128)(2,1)} %param.21, bf16[128,512,128]{2,1,0:T(8,128)(2,1)} %gather_fusion.4, pred[128]{0:T(512)(128)(4,1)S(1)} %get-tuple-element.16, bf16[128,512,128]{1,2,0:T(8,128)(2,1)} %gather_fusion.3, ...), kind=kOutput, calls=%fused_computation.24 | convolution fusion | flops 2172649472 | bytes 50331904 | tf_op jit(solution)/shard_map/wsx,wsy->sxy/dot_general | solution.py:53
  (37 shorter events, 3.7 us)
Async XLA Ops:
  7.2 29.9 %copy-start = (bf16[512,512]{1,0:T(8,128)(2,1)S(1)}, bf16[512,512]{1,0:T(8,128)(2,1)}, u32[]{:S(2)}) copy-start(bf16[512,512]{1,0:T(8,128)(2,1)} %param.17) | copy-start | bytes 1572868
  7.2 205.8 %copy-start.3 = (s32[1,1,128]{2,1,0:T(1,128)S(1)}, s32[1,1,128]{2,1,0:T(1,128)}, u32[]{:S(2)}) copy-start(s32[1,1,128]{2,1,0:T(1,128)} %param.23) | copy-start | bytes 1540
  7.2 205.8 %copy-start.4 = (s32[1,1,128]{2,1,0:T(1,128)S(1)}, s32[1,1,128]{2,1,0:T(1,128)}, u32[]{:S(2)}) copy-start(s32[1,1,128]{2,1,0:T(1,128)} %param.22) | copy-start | bytes 1540
  7.2 205.8 %copy-start.5 = (s32[1,1,128]{2,1,0:T(1,128)S(1)}, s32[1,1,128]{2,1,0:T(1,128)}, u32[]{:S(2)}) copy-start(s32[1,1,128]{2,1,0:T(1,128)} %param.25) | copy-start | bytes 1540
  7.2 205.8 %copy-start.6 = (s32[1,1,128]{2,1,0:T(1,128)S(1)}, s32[1,1,128]{2,1,0:T(1,128)}, u32[]{:S(2)}) copy-start(s32[1,1,128]{2,1,0:T(1,128)} %param.24) | copy-start | bytes 1540
  7.2 29.8 %all-gather.7.cloned.1.call-start = ((), (), s32[]{:S(2)}) async-start(), calls=%async_computation | async-start | bytes 1179648 | tf_op jit(solution)/shard_map/all_gather | solution.py:10
  8.0 177.1 %all-reduce.2.cloned.1.call-start = ((), (), s32[]{:S(2)}) async-start(), calls=%async_computation.1 | async-start | bytes 262144 | tf_op jit(solution)/shard_map/psum | solution.py:26
  39.0 151.7 %copy-start.2 = (bf16[512,1024]{1,0:T(8,128)(2,1)}, bf16[512,1024]{1,0:T(8,128)(2,1)S(1)}, u32[]{:S(2)}) copy-start(bf16[512,1024]{1,0:T(8,128)(2,1)S(1)} %convolution_convert_fusion.1) | copy-start | bytes 3145732
  40.0 170.1 %all-gather.9.cloned.1.call-start = ((), (), s32[]{:S(2)}) async-start(), calls=%async_computation.2 | async-start | bytes 1179648 | tf_op jit(solution)/shard_map/all_gather | solution.py:10
  187.5 108.4 %all-gather.11.cloned.1.call-start = ((), (), s32[]{:S(2)}) async-start(), calls=%async_computation.3 | async-start | bytes 4325376 | tf_op jit(solution)/shard_map/all_gather | solution.py:43
  190.5 186.4 %all-gather.13.cloned.1.call-start = ((), (), s32[]{:S(2)}) async-start(), calls=%async_computation.4 | async-start | bytes 4325376 | tf_op jit(solution)/shard_map/all_gather | solution.py:43
  393.8 18.2 %copy-start.1 = (bf16[512,512]{1,0:T(8,128)(2,1)S(1)}, bf16[512,512]{1,0:T(8,128)(2,1)}, u32[]{:S(2)}) copy-start(bf16[512,512]{1,0:T(8,128)(2,1)} %param.17) | copy-start | bytes 1572868
Sparse Core Ops, SparseCore 0:
  9.9 27.1 all-gather.6
  41.1 143.9 all-reduce.1
  187.6 22.4 all-gather.8
  212.6 83.2 all-gather.10
  298.3 78.5 all-gather.12
where the time goes:
time: 419 us
  waiting for transfers between devices  294 us (70%)
  local copies, waits for them, and re-layouts  61.9 us (15%)
  matrix products  41.4 us (10%)
  between operations  16.6 us (4%)
    psum x1, waiting for transfers between devices, bridge_columns(): lax.psum(jnp.where(owned_here, column_piece.astype(jnp.float32), 0.0).ast...  139 us
    all_gather x2, waiting for transfers between devices, gather_tiles(): lax.all_gather(pick_tiles(lower_full, block_size), 'row', axis=1, tiled=T...  111 us
    all_gather x2, waiting for transfers between devices, factor_panel(): lax.all_gather(panel_part, 'col', axis=0, tiled=True)  43.8 us
    dot_general x2, matrix products, schur_terms(): jnp.einsum('wsx,wsy->sxy', left_tiles, right_tiles, preferred_element_typ...  35 us
    gather x2, local copies, waits for them, and re-layouts, schur_terms(): jnp.take(column_set, slot_cols.reshape(-1) // lax.axis_size('col'), axis=1)  21.1 us
    gather x2, local copies, waits for them, and re-layouts, schur_terms(): jnp.take(local_blocks, slot_rows.reshape(-1) % local_count, axis=1)  16.5 us
    reshape x2, local copies, waits for them, and re-layouts, schur_terms(): column_set = tiles.reshape(panel_width, -1, block_size)  12.8 us
  transfers between devices with their start and end apart: 5, of which 5 were waited for; matrix products, arithmetic and copies ran while one was open for 16% of the time, Pallas kernels for 0%

commit v1 on v0

--- a/solution.py
+++ b/solution.py
@@ -23,8 +23,11 @@
     )
     owner_row = chosen // local_count
     owned_here = owner_row == lax.axis_index("row")
-    summed = lax.psum(
-        jnp.where(owned_here, column_piece.astype(jnp.float32), 0.0).astype(jnp.bfloat16), "row"
+    summed = jnp.sum(
+        lax.all_gather(
+            jnp.where(owned_here, column_piece.astype(jnp.float32), 0.0).astype(jnp.bfloat16), "row"
+        ),
+        axis=0,
     )
     return summed
 

time: 419 us -> 359 us (0.86)
  waiting for transfers between devices: 294 us -> 231 us
    psum x1 -> x0, waiting for transfers between devices: 139 us -> none  [bridge_columns(): lax.psum(jnp.where(owned_here, column_piece.astype(jnp.float32), 0.0).ast...]
    all_gather x0 -> x1, waiting for transfers between devices: none -> 76.2 us  [bridge_columns(): lax.all_gather(jnp.where(owned_here, column_piece.astype(jnp.float32), 0....]
  transfers between devices with their start and end apart: 5 -> 5, of which waited for: 5 -> 5; matrix products, arithmetic and copies ran while one was open for 16% -> 19% of each run, Pallas kernels for 0% -> 0%
where the time goes in v1:
time: 359 us; the launch traced here: 358 us
  waiting for transfers between devices  231 us (64%)
  local copies, waits for them, and re-layouts  61.9 us (17%)
  matrix products  41.3 us (12%)
  between operations  16.6 us (5%)
  other arithmetic  7.06 us (2%)
    all_gather x2, waiting for transfers between devices, gather_tiles(): lax.all_gather(pick_tiles(lower_full, block_size), 'row', axis=1, tiled=T...  111 us
    all_gather x1, waiting for transfers between devices, bridge_columns(): lax.all_gather(jnp.where(owned_here, column_piece.astype(jnp.float32), 0....  76.2 us
    all_gather x2, waiting for transfers between devices, factor_panel(): lax.all_gather(panel_part, 'col', axis=0, tiled=True)  43.1 us
    dot_general x2, matrix products, schur_terms(): jnp.einsum('wsx,wsy->sxy', left_tiles, right_tiles, preferred_element_typ...  35 us
    gather x2, local copies, waits for them, and re-layouts, schur_terms(): jnp.take(column_set, slot_cols.reshape(-1) // lax.axis_size('col'), axis=1)  21.1 us
    gather x2, local copies, waits for them, and re-layouts, schur_terms(): jnp.take(local_blocks, slot_rows.reshape(-1) % local_count, axis=1)  16.5 us
    reshape x2, local copies, waits for them, and re-layouts, schur_terms(): column_set = tiles.reshape(panel_width, -1, block_size)  12.8 us
  transfers between devices with their start and end apart: 5, of which 5 were waited for; matrix products, arithmetic and copies ran while one was open for 19% of the time, Pallas kernels for 0%

profile of v1, /device:TPU:2, one launch (start us, length us, event | category | flops | bytes accessed | tf_op | source)
XLA Modules:
  0.0 358.4 jit_solution(6116448207912589067)
XLA Ops:
  8.0 1.2 dynamic_slice.20
  11.9 25.2 %all-gather.9.cloned.1.call-done = bf16[512,1024]{1,0:T(8,128)(2,1)} async-done(((bf16[64,1024]{1,0:T(8,128)(2,1)}), bf16[512,1024]{1,0:T(8,128)(2,1)}) %all-gather.9.cloned.1.call-update) | async-done | bytes 1048592 | tf_op jit(solution)/shard_map/all_gather | solution.py:10
  37.1 1.9 convolution_convert_fusion.1
  41.0 1.7 gather_fusion
  42.6 2.3 copy.22
  44.9 2.4 bitcast_select_fusion
  47.3 76.2 %all-gather.13.cloned.1.call-done = bf16[16384,64]{1,0:T(8,128)(2,1)} async-done(((bf16[512,64]{1,0:T(8,128)(2,1)}), bf16[16384,64]{1,0:T(8,128)(2,1)}) %all-gather.13.cloned.1.call-update) | async-done | bytes 2097168 | tf_op jit(solution)/shard_map/all_gather | solution.py:27
  123.5 3.0 reduce_sum.12
  126.5 2.3 fusion.23
  129.0 1.3 copy.30
  130.3 1.6 constant_dynamic-slice_fusion.1
  132.1 17.9 %all-gather.11.cloned.1.call-done = bf16[512,1024]{1,0:T(8,128)(2,1)} async-done(((bf16[64,1024]{1,0:T(8,128)(2,1)}), bf16[512,1024]{1,0:T(8,128)(2,1)}) %all-gather.11.cloned.1.call-update) | async-done | bytes 1048592 | tf_op jit(solution)/shard_map/all_gather | solution.py:10
  150.0 2.0 convolution_convert_fusion
  152.8 8.2 %gather_fusion.1 = bf16[128,512,128]{2,1,0:T(8,128)(2,1)} fusion(bf16[512,8,128]{2,0,1:T(8,128)(2,1)S(1)} %copy_bitcast_fusion, s32[1024]{0:T(1024)S(1)} %pad_clamp_fusion.3), kind=kCustom, calls=%fused_computation.clone | custom fusion | bytes 33554944 | tf_op jit(solution)/shard_map/jit(_take)/gather | solution.py:54
  161.1 1.6 constant_dynamic-slice_fusion.2
  163.6 8.2 %gather_fusion.3 = bf16[128,512,128]{1,2,0:T(8,128)(2,1)} fusion(bf16[512,8,128]{0,2,1:T(8,128)(2,1)S(1)} %bitcast.78, s32[1024]{0:T(1024)S(1)} %pad_clamp_fusion.1), kind=kCustom, calls=%fused_computation.2.clone | custom fusion | bytes 33554944 | tf_op jit(solution)/shard_map/jit(_take)/gather | solution.py:54
  171.8 64.0 %all-gather.15.cloned.1.call-done = bf16[512,1,1,4096]{0,3,2,1:T(8,128)(2,1)} async-done(((bf16[512,1,1,128]{0,3,2,1:T(8,128)(2,1)}), bf16[512,1,1,4096]{0,3,2,1:T(8,128)(2,1)}) %all-gather.15.cloned.1.call-update) | async-done | bytes 4194320 | tf_op jit(solution)/shard_map/all_gather | solution.py:46
  235.8 6.4 %copy.25 = bf16[512,32,128]{2,0,1:T(8,128)(2,1)} copy(bf16[512,32,128]{0,2,1:T(8,128)(2,1)} %bitcast.80) | data formatting | bytes 8388608 | tf_op jit(solution)/shard_map/reshape | solution.py:52
  242.2 10.6 %gather_fusion.2 = bf16[128,512,128]{2,1,0:T(8,128)(2,1)} fusion(bf16[512,32,128]{2,0,1:T(8,128)(2,1)} %copy.25, s32[1024]{0:T(1024)S(1)} %pad_clamp_fusion.2), kind=kCustom, calls=%fused_computation.1.clone | custom fusion | bytes 33554944 | tf_op jit(solution)/shard_map/jit(_take)/gather | solution.py:55
  252.8 16.8 %fusion.3 = f32[128,128,128]{2,1,0:T(8,128)} fusion(bf16[128,512,128]{2,1,0:T(8,128)(2,1)} %gather_fusion.2, bf16[128,512,128]{2,1,0:T(8,128)(2,1)} %gather_fusion.1, pred[128]{0:T(512)(128)(4,1)S(1)} %get-tuple-element.20, pred[128]{0:T(512)(128)(4,1)S(1)} %get-tuple-element.26), kind=kOutput, calls=%fused_computation.8 | convolution fusion | flops 2164260864 | bytes 41943296 | tf_op jit(solution)/shard_map/wsx,wsy->sxy/dot_general | solution.py:56
  269.6 47.2 %all-gather.17.cloned.1.call-done = bf16[512,1,1,4096]{0,3,2,1:T(8,128)(2,1)} async-done(((bf16[512,1,1,128]{0,3,2,1:T(8,128)(2,1)}), bf16[512,1,1,4096]{0,3,2,1:T(8,128)(2,1)}) %all-gather.17.cloned.1.call-update) | async-done | bytes 4194320 | tf_op jit(solution)/shard_map/all_gather | solution.py:46
  316.8 6.4 %copy.27 = bf16[512,32,128]{2,0,1:T(8,128)(2,1)} copy(bf16[512,32,128]{0,2,1:T(8,128)(2,1)} %bitcast.81) | data formatting | bytes 8388608 | tf_op jit(solution)/shard_map/reshape | solution.py:52
  323.2 10.5 %gather_fusion.4 = bf16[128,512,128]{2,1,0:T(8,128)(2,1)} fusion(bf16[512,32,128]{2,0,1:T(8,128)(2,1)} %copy.27, s32[1024]{0:T(1024)S(1)} %pad_clamp_fusion), kind=kCustom, calls=%fused_computation.3.clone | custom fusion | bytes 33554944 | tf_op jit(solution)/shard_map/jit(_take)/gather | solution.py:55
  333.7 18.2 %fusion.18 = bf16[1,1,128,128,128]{4,3,2,1,0:T(8,128)(2,1)} fusion(f32[128,128,128]{2,1,0:T(8,128)} %fusion.3, bf16[1,1,128,128,128]{4,3,2,1,0:T(8,128)(2,1)} %param.21, bf16[128,512,128]{2,1,0:T(8,128)(2,1)} %gather_fusion.4, pred[128]{0:T(512)(128)(4,1)S(1)} %get-tuple-element.16, bf16[128,512,128]{1,2,0:T(8,128)(2,1)} %gather_fusion.3, ...), kind=kOutput, calls=%fused_computation.24 | convolution fusion | flops 2172649472 | bytes 50331904 | tf_op jit(solution)/shard_map/wsx,wsy->sxy/dot_general | solution.py:56
  (40 shorter events, 4.6 us)
Async XLA Ops:
  7.2 29.9 %copy-start = (bf16[512,512]{1,0:T(8,128)(2,1)S(1)}, bf16[512,512]{1,0:T(8,128)(2,1)}, u32[]{:S(2)}) copy-start(bf16[512,512]{1,0:T(8,128)(2,1)} %param.17) | copy-start | bytes 1572868
  7.2 142.8 %copy-start.7 = (bf16[512,512]{1,0:T(8,128)(2,1)S(1)}, bf16[512,512]{1,0:T(8,128)(2,1)}, u32[]{:S(2)}) copy-start(bf16[512,512]{1,0:T(8,128)(2,1)} %param.18) | copy-start | bytes 1572868
  7.2 145.5 %copy-start.3 = (s32[1,1,128]{2,1,0:T(1,128)S(1)}, s32[1,1,128]{2,1,0:T(1,128)}, u32[]{:S(2)}) copy-start(s32[1,1,128]{2,1,0:T(1,128)} %param.23) | copy-start | bytes 1540
  7.2 145.5 %copy-start.4 = (s32[1,1,128]{2,1,0:T(1,128)S(1)}, s32[1,1,128]{2,1,0:T(1,128)}, u32[]{:S(2)}) copy-start(s32[1,1,128]{2,1,0:T(1,128)} %param.22) | copy-start | bytes 1540
  7.2 145.6 %copy-start.5 = (s32[1,1,128]{2,1,0:T(1,128)S(1)}, s32[1,1,128]{2,1,0:T(1,128)}, u32[]{:S(2)}) copy-start(s32[1,1,128]{2,1,0:T(1,128)} %param.25) | copy-start | bytes 1540
  7.2 145.6 %copy-start.6 = (s32[1,1,128]{2,1,0:T(1,128)S(1)}, s32[1,1,128]{2,1,0:T(1,128)}, u32[]{:S(2)}) copy-start(s32[1,1,128]{2,1,0:T(1,128)} %param.24) | copy-start | bytes 1540
  7.2 29.8 %all-gather.9.cloned.1.call-start = ((), (), s32[]{:S(2)}) async-start(), calls=%async_computation | async-start | bytes 1179648 | tf_op jit(solution)/shard_map/all_gather | solution.py:10
  8.0 115.6 %all-gather.13.cloned.1.call-start = ((), (), s32[]{:S(2)}) async-start(), calls=%async_computation.2 | async-start | bytes 4325376 | tf_op jit(solution)/shard_map/all_gather | solution.py:27
  39.0 93.1 %copy-start.2 = (bf16[512,1024]{1,0:T(8,128)(2,1)}, bf16[512,1024]{1,0:T(8,128)(2,1)S(1)}, u32[]{:S(2)}) copy-start(bf16[512,1024]{1,0:T(8,128)(2,1)S(1)} %convolution_convert_fusion.1) | copy-start | bytes 3145732
  40.0 110.1 %all-gather.11.cloned.1.call-start = ((), (), s32[]{:S(2)}) async-start(), calls=%async_computation.1 | async-start | bytes 1179648 | tf_op jit(solution)/shard_map/all_gather | solution.py:10
  128.9 106.9 %all-gather.15.cloned.1.call-start = ((), (), s32[]{:S(2)}) async-start(), calls=%async_computation.3 | async-start | bytes 4325376 | tf_op jit(solution)/shard_map/all_gather | solution.py:46
  131.9 184.9 %all-gather.17.cloned.1.call-start = ((), (), s32[]{:S(2)}) async-start(), calls=%async_computation.4 | async-start | bytes 4325376 | tf_op jit(solution)/shard_map/all_gather | solution.py:46
  333.7 18.2 %copy-start.1 = (bf16[512,512]{1,0:T(8,128)(2,1)S(1)}, bf16[512,512]{1,0:T(8,128)(2,1)}, u32[]{:S(2)}) copy-start(bf16[512,512]{1,0:T(8,128)(2,1)} %param.17) | copy-start | bytes 1572868
Sparse Core Ops, SparseCore 0:
  9.9 27.1 all-gather.8
  40.2 83.2 all-gather.12
  129.0 20.9 all-gather.10
  152.5 83.2 all-gather.14
  238.2 78.5 all-gather.16
